TPU v7x, 256 devices: a whole 4x4x8 slice. The times are simulated.
256 devices in a mesh: tensor: 8 (over z_hi, core), mirror: 2 (over z_lo), dp: 16 (over x, y).
Axes of the slice: x: 4, y: 4, z: 8 (z_hi: 4, z_lo: 2; z = z_hi * 2 + z_lo), core: 2. Of those that a mesh axis runs over, the one named last changes fastest.
Arguments:
- layer_input: bfloat16 [32, 256, 4096], P(('mirror', 'dp'), 'tensor'), may hold values from -6 to 6
- qk_weight: bfloat16 [4096, 2, 4096], P(None, None, 'tensor'), may hold values from -0.09375 to 0.09375
- query_proj: bfloat16 [32, 256, 4096], P(('mirror', 'dp'), None, 'tensor'), may hold values from -24 to 24
- key_proj: bfloat16 [32, 256, 4096], P(('mirror', 'dp'), None, 'tensor'), may hold values from -24 to 24
- value_proj: bfloat16 [32, 256, 4096], P(('mirror', 'dp'), None, 'tensor'), may hold values from -6 to 6
- head_grad: bfloat16 [32, 256, 4096], P(('mirror', 'dp'), None, 'tensor'), may hold values from -6 to 6
- doc_ids: int32 [32, 256], P(('mirror', 'dp')), may hold values from 0 to 3, as said below
Outputs:
- input_grad: bfloat16 [32, 256, 4096], P(('mirror', 'dp'), 'tensor')
- qk_weight_grad: float32 [4096, 2, 4096], P(('mirror', 'dp'), None, 'tensor')
Inputs may be any that keep to these rules, and one draw needn't show every extreme that they name: `doc_ids`: within each sequence of 128 tokens the ids start at 0, never fall, and each of the four documents holds a multiple of 8 tokens.
All inputs are finite; a program needn't handle non-finite values.
Results may differ from a plain program's by a relative error of at most 0.023.
Values may be sent and summed in bfloat16 or wider, within the bound.
A program may use at most 128 MiB of HBM per device.

v0:
```python
import math
import jax
import jax.numpy as jnp
from jax import lax
from jax.sharding import PartitionSpec as P

HD = 128
SEQ = 128


def rotate_pairs(values, cosine, sine_table):
    half = values.shape[-1] // 2
    first_half = values[..., :half]
    second_half = values[..., half:]
    cos_b = cosine[None, :, None, :]
    sin_b = sine_table[None, :, None, :]
    return jnp.concatenate(
        [first_half * cos_b - second_half * sin_b, second_half * cos_b + first_half * sin_b],
        axis=-1,
    )


def unrotate_pairs(values, cosine, sine_table):
    half = values.shape[-1] // 2
    first_half = values[..., :half]
    second_half = values[..., half:]
    cos_b = cosine[None, :, None, :]
    sin_b = sine_table[None, :, None, :]
    return jnp.concatenate(
        [first_half * cos_b + second_half * sin_b, second_half * cos_b - first_half * sin_b],
        axis=-1,
    )


def attention_grads(query_rows, key_rows, value_rows, grad_rows, doc_row):
    token_count, full_width = query_rows.shape
    head_count = full_width // HD
    micro_count = token_count // SEQ
    shape_four = (micro_count, SEQ, head_count, HD)
    positions = jnp.arange(SEQ).astype(jnp.float32)
    inverse = jnp.exp(-(2.0 * jnp.arange(HD // 2).astype(jnp.float32) / HD) * math.log(10000.0))
    angles = positions[:, None] * inverse[None, :]
    cosine = jnp.cos(angles)
    sine_table = jnp.sin(angles)
    q_rot = rotate_pairs(
        query_rows.reshape(shape_four).astype(jnp.float32), cosine, sine_table
    ).astype(jnp.bfloat16)
    k_rot = rotate_pairs(
        key_rows.reshape(shape_four).astype(jnp.float32), cosine, sine_table
    ).astype(jnp.bfloat16)
    scale = 1.0 / math.sqrt(HD)
    scores = jnp.einsum("bshd,bthd->bhst", q_rot, k_rot, preferred_element_type=jnp.float32) * scale
    docs = doc_row.reshape(micro_count, SEQ)
    index_seq = jnp.arange(SEQ)
    causal = index_seq[None, :] <= index_seq[:, None]
    allowed = causal[None, :, :] & (docs[:, :, None] == docs[:, None, :])
    scores = jnp.where(allowed[:, None, :, :], scores, -1e30)
    highest = jnp.max(scores, axis=-1, keepdims=True)
    exps = jnp.exp(scores - highest)
    probs = exps / jnp.sum(exps, axis=-1, keepdims=True)
    dprob = jnp.einsum(
        "bshd,bthd->bhst",
        grad_rows.reshape(shape_four),
        value_rows.reshape(shape_four),
        preferred_element_type=jnp.float32,
    )
    delta = jnp.sum(probs * dprob, axis=-1, keepdims=True)
    dscore = (probs * (dprob - delta)).astype(jnp.bfloat16)
    dq_rot = (
        jnp.einsum("bhst,bthd->bshd", dscore, k_rot, preferred_element_type=jnp.float32) * scale
    )
    dk_rot = (
        jnp.einsum("bhst,bshd->bthd", dscore, q_rot, preferred_element_type=jnp.float32) * scale
    )
    query_grad = (
        unrotate_pairs(dq_rot, cosine, sine_table)
        .astype(jnp.bfloat16)
        .reshape(token_count, full_width)
    )
    key_grad = (
        unrotate_pairs(dk_rot, cosine, sine_table)
        .astype(jnp.bfloat16)
        .reshape(token_count, full_width)
    )
    return (query_grad, key_grad)


def shards(layer_input, qk_weight, query_proj, key_proj, value_proj, head_grad, doc_ids):
    tensor_count = lax.axis_size("tensor")
    mirror_count = lax.axis_size("mirror")
    data_count = lax.axis_size("dp")
    replicas = mirror_count * data_count
    token_count = query_proj.shape[1]
    group_width = query_proj.shape[2]
    model_width = layer_input.shape[2]
    block_rows = model_width // replicas
    query_grad, key_grad = attention_grads(
        query_proj[0], key_proj[0], value_proj[0], head_grad[0], doc_ids[0]
    )
    grad_pair = jnp.concatenate([query_grad, key_grad], axis=1)
    weight_flat = qk_weight.reshape(model_width, 2 * group_width)
    summed_input = lax.psum_scatter(
        lax.dot_general(
            grad_pair, weight_flat, (((1,), (1,)), ((), ())), preferred_element_type=jnp.float32
        ).astype(jnp.bfloat16),
        "tensor",
        scatter_dimension=0,
        tiled=True,
    )
    input_grad = summed_input.reshape(1, token_count // tensor_count, model_width)
    gathered = lax.all_gather(layer_input, "tensor", axis=1, tiled=True)[0]
    summed = lax.psum_scatter(
        lax.dot_general(
            gathered, grad_pair, (((0,), (0,)), ((), ())), preferred_element_type=jnp.float32
        ).astype(jnp.bfloat16),
        ("mirror", "dp"),
        scatter_dimension=0,
        tiled=True,
    ).astype(jnp.float32)
    weight_grad = (summed / replicas).reshape(block_rows, 2, group_width)
    return (input_grad, weight_grad)


def solution(mesh):
    in_specs = (
        P(("mirror", "dp"), "tensor", None),
        P(None, None, "tensor"),
        P(("mirror", "dp"), None, "tensor"),
        P(("mirror", "dp"), None, "tensor"),
        P(("mirror", "dp"), None, "tensor"),
        P(("mirror", "dp"), None, "tensor"),
        P(("mirror", "dp"), None),
    )
    out_specs = (P(("mirror", "dp"), "tensor", None), P(("mirror", "dp"), None, "tensor"))
    return jax.shard_map(shards, mesh=mesh, in_specs=in_specs, out_specs=out_specs, check_vma=False)
```

profile of v0, /device:TPU:8, one launch (start us, length us, event | category | flops | bytes accessed | tf_op | source)
XLA Modules:
  0.0 301.0 jit_solution(3463841190845136703)
XLA Ops:
  7.2 0.7 all-gather.2.cloned.1.call-update
  7.9 1.1 reshape.110
  9.1 1.1 reshape.111
  10.2 1.0 reshape_squeeze.9
  11.2 1.0 reshape_squeeze.8
  12.3 0.9 compare_and_fusion
  13.1 0.3 multiply_cosine_fusion
  13.4 0.6 fusion.18
  14.1 0.3 subtract_convert_fusion.3
  14.4 0.5 fusion.20
  14.9 0.3 multiply_reduce_fusion
  15.3 0.3 fusion.4
  15.6 0.4 fusion.5
  16.0 0.5 add_convert_fusion
  17.2 31.7 %all-gather.2.cloned.1.call-done = bf16[1,256,4096]{2,1,0:T(8,128)(2,1)} async-done(((bf16[1,32,4096]{2,1,0:T(8,128)(2,1)}), bf16[1,256,4096]{2,1,0:T(8,128)(2,1)}) %all-gather.2.cloned.1.call-update) | async-done | bytes 2097168 | tf_op jit(solution)/shard_map/all_gather | solution.py:111
  49.0 7.2 %convert_bitcast_fusion = bf16[4096,1024]{0,1:T(8,128)(2,1)} fusion(bf16[256,1024]{1,0:T(8,128)(2,1)S(1)} %bitcast_dynamic-update-slice_fusion, bf16[1,256,4096]{2,1,0:T(8,128)(2,1)} %all-gather.2.cloned.1.call-done), kind=kOutput, calls=%fused_computation.1 | convolution fusion | flops 2151677952 | bytes 11010048 | tf_op jit(solution)/shard_map/dot_general | solution.py:113
  56.2 12.0 %copy.54 = bf16[4096,1024]{1,0:T(8,128)(2,1)} copy(bf16[4096,1024]{0,1:T(8,128)(2,1)} %convert_bitcast_fusion) | data formatting | bytes 16777216
  68.2 0.2 reduce-scatter.5.cloned.1.call-start
  68.4 9.3 %copy.62 = bf16[512,8,2,512]{3,1,2,0:T(8,128)(2,1)} copy(bf16[512,8,2,512]{3,2,1,0:T(2,128)(2,1)} %bitcast.28) | data formatting | bytes 16777216
  77.7 7.1 %convolution_convert_fusion = bf16[256,4096]{1,0:T(8,128)(2,1)} fusion(bf16[256,1024]{1,0:T(8,128)(2,1)S(1)} %bitcast_dynamic-update-slice_fusion, bf16[4096,1024]{1,0:T(8,128)(2,1)} %bitcast.29), kind=kOutput, calls=%fused_computation.2 | convolution fusion | flops 2148532224 | bytes 11010048 | tf_op jit(solution)/shard_map/dot_general | solution.py:103
  84.9 160.5 %reduce-scatter.7.cloned.1.call-done = bf16[128,1024]{1,0:T(8,128)(2,1)} async-done(((bf16[4096,1024]{1,0:T(8,128)(2,1)}), bf16[128,1024]{1,0:T(8,128)(2,1)}) %reduce-scatter.7.cloned.1.call-update) | async-done | bytes 262160
  245.3 1.1 copy.55
  246.5 1.0 copy.47
  247.5 47.0 %reduce-scatter.5.cloned.1.call-done = bf16[32,4096]{1,0:T(8,128)(2,1)} async-done(((bf16[256,4096]{1,0:T(8,128)(2,1)}), bf16[32,4096]{1,0:T(8,128)(2,1)}) %reduce-scatter.5.cloned.1.call-update) | async-done | bytes 262160 | tf_op jit(solution)/shard_map/reduce_scatter | solution.py:102
  (15 shorter events, 1.0 us)
Async XLA Ops:
  7.2 41.8 %all-gather.2.cloned.1.call-start = ((), (), s32[]{:S(2)}) async-start(), calls=%async_computation.3 | async-start | bytes 2359296 | tf_op jit(solution)/shard_map/all_gather | solution.py:111
  7.9 237.4 %reduce-scatter.7.cloned.1.call-start = ((), (), s32[]{:S(2)}) async-start(), calls=%async_computation.4 | async-start | bytes 8650752
  68.2 226.3 %reduce-scatter.5.cloned.1.call-start = ((), (), s32[]{:S(2)}) async-start(), calls=%async_computation.2 | async-start | bytes 2359296 | tf_op jit(solution)/shard_map/reduce_scatter | solution.py:102
Sparse Core Ops, SparseCore 0:
  9.8 39.0 all-gather.1
  68.3 176.9 reduce-scatter.6
  248.5 46.0 reduce-scatter.4
where the time goes:
time: 302 us; the launch traced here: 301 us
  waiting for transfers between devices  240 us (79%)
  local copies, waits for them, and re-layouts  28.7 us (10%)
  matrix products  15.8 us (5%)
  between operations  13.9 us (5%)
    unnamed x4, waiting for transfers between devices  161 us
    reduce_scatter x1, waiting for transfers between devices, shards(): lax.psum_scatter(lax.dot_general(grad_pair, weight_flat, (((1,), (1,)), (...  47 us
    all_gather x1, waiting for transfers between devices, shards(): gathered = lax.all_gather(layer_input, 'tensor', axis=1, tiled=True)[0]  31.7 us
    unnamed x5, local copies, waits for them, and re-layouts  23.4 us
    dot_general x1, matrix products, shards(): lax.dot_general(gathered, grad_pair, (((0,), (0,)), ((), ())), preferred_...  7.19 us
    dot_general x1, matrix products, shards(): lax.dot_general(grad_pair, weight_flat, (((1,), (1,)), ((), ())), preferr...  7.14 us
  transfers between devices with their start and end apart: 3, of which 3 were waited for; matrix products, arithmetic and copies ran while one was open for 9% of the time, Pallas kernels for 0%

commit v1 on v0

--- a/solution.py
+++ b/solution.py
@@ -108,7 +108,9 @@
         tiled=True,
     )
     input_grad = summed_input.reshape(1, token_count // tensor_count, model_width)
-    gathered = lax.all_gather(layer_input, "tensor", axis=1, tiled=True)[0]
+    gathered = jnp.concatenate(
+        lax.all_to_all(jnp.stack([layer_input] * lax.axis_size("tensor")), "tensor", 0, 0), axis=1
+    )[0]
     summed = lax.psum_scatter(
         lax.dot_general(
             gathered, grad_pair, (((0,), (0,)), ((), ())), preferred_element_type=jnp.float32

time: 302 us -> 320 us (1.060)
  starting transfers between devices: 0.3 us -> 8.72 us
  waiting for transfers between devices: 240 us -> 244 us
    all_to_all x0 -> x1, waiting for transfers between devices: none -> 38.3 us  [shards(): lax.all_to_all(jnp.stack([layer_input] * lax.axis_size('tensor')), 'tenso...]
    all_gather x1 -> x0, waiting for transfers between devices: 31.7 us -> none  [shards(): gathered = lax.all_gather(layer_input, 'tensor', axis=1, tiled=True)[0]]
    all_to_all x0 -> x1, starting transfers between devices: none -> 8.47 us  [shards(): lax.all_to_all(jnp.stack([layer_input] * lax.axis_size('tensor')), 'tenso...]
    unnamed x4 -> x3, waiting for transfers between devices: 161 us -> 159 us
    unnamed x5 -> x11, local copies, waits for them, and re-layouts: 23.4 us -> 23.5 us
  transfers between devices with their start and end apart: 3 -> 3, of which waited for: 3 -> 3; matrix products, arithmetic and copies ran while one was open for 9% -> 10% of each run, Pallas kernels for 0% -> 0%
where the time goes in v1:
time: 320 us; the launch traced here: 319 us
  waiting for transfers between devices  244 us (76%)
  local copies, waits for them, and re-layouts  31.8 us (10%)
  matrix products  16.8 us (5%)
  between operations  14.2 us (4%)
  starting transfers between devices  8.72 us (3%)
  other arithmetic  3.27 us (1%)
    unnamed x3, waiting for transfers between devices  159 us
    reduce_scatter x1, waiting for transfers between devices, shards(): lax.psum_scatter(lax.dot_general(grad_pair, weight_flat, (((1,), (1,)), (...  47.3 us
    all_to_all x1, waiting for transfers between devices, shards(): lax.all_to_all(jnp.stack([layer_input] * lax.axis_size('tensor')), 'tenso...  38.3 us
    unnamed x11, local copies, waits for them, and re-layouts  23.5 us
    all_to_all x1, starting transfers between devices, shards(): lax.all_to_all(jnp.stack([layer_input] * lax.axis_size('tensor')), 'tenso...  8.47 us
    dot_general x1, matrix products, shards(): lax.dot_general(grad_pair, weight_flat, (((1,), (1,)), ((), ())), preferr...  7.11 us
  transfers between devices with their start and end apart: 3, of which 3 were waited for; matrix products, arithmetic and copies ran while one was open for 10% of the time, Pallas kernels for 0%

profile of v1, /device:TPU:8, one launch (start us, length us, event | category | flops | bytes accessed | tf_op | source)
XLA Modules:
  0.0 319.3 jit_solution(17610878486404545350)
XLA Ops:
  7.2 2.6 stack.2
  9.8 8.5 %all-to-all-start = ((bf16[8,1,32,4096]{3,2,1,0:T(8,128)(2,1)}), bf16[8,1,32,4096]{3,2,1,0:T(8,128)(2,1)S(1)}, u32[]{:S(2)}, u32[]{:S(2)}) async-start(bf16[8,1,32,4096]{3,2,1,0:T(8,128)(2,1)} %stack.2), calls=%async_computation.1 | async-start | bytes 4194304 | tf_op jit(solution)/shard_map/all_to_all | solution.py:112
  18.3 1.1 reshape.113
  19.4 1.1 reshape.114
  20.5 1.7 reshape_squeeze.9
  22.2 0.8 reshape_squeeze.8
  23.1 0.7 compare_and_fusion
  23.8 0.3 multiply_cosine_fusion
  24.1 0.6 fusion.17
  24.7 0.3 subtract_convert_fusion.3
  25.0 2.0 fusion.19
  27.0 1.4 multiply_reduce_fusion
  28.5 1.1 multiply_convert_fusion
  29.9 0.4 fusion.4
  30.3 0.5 add_convert_fusion
  31.6 38.3 %all-to-all-done = bf16[8,1,32,4096]{3,2,1,0:T(8,128)(2,1)S(1)} async-done(((bf16[8,1,32,4096]{3,2,1,0:T(8,128)(2,1)}), bf16[8,1,32,4096]{3,2,1,0:T(8,128)(2,1)S(1)}, u32[]{:S(2)}, u32[]{:S(2)}) %all-to-all-start) | async-done | bytes 2097184 | tf_op jit(solution)/shard_map/all_to_all | solution.py:112
  69.9 5.6 %convert_bitcast_fusion = bf16[4096,1024]{0,1:T(8,128)(2,1)} fusion(bf16[256,1024]{1,0:T(8,128)(2,1)S(1)} %bitcast_dynamic-update-slice_fusion, bf16[256,4096]{1,0:T(8,128)(2,1)S(1)} %bitcast.30), kind=kOutput, calls=%fused_computation.1 | convolution fusion | flops 2151677952 | bytes 11010048 | tf_op jit(solution)/shard_map/dot_general | solution.py:115
  75.5 12.0 %copy.54 = bf16[4096,1024]{1,0:T(8,128)(2,1)} copy(bf16[4096,1024]{0,1:T(8,128)(2,1)} %convert_bitcast_fusion) | data formatting | bytes 16777216
  87.7 9.3 %copy.62 = bf16[512,8,2,512]{3,1,2,0:T(8,128)(2,1)} copy(bf16[512,8,2,512]{3,2,1,0:T(2,128)(2,1)} %bitcast.28) | data formatting | bytes 16777216
  97.0 7.1 %convolution_convert_fusion = bf16[256,4096]{1,0:T(8,128)(2,1)} fusion(bf16[256,1024]{1,0:T(8,128)(2,1)S(1)} %bitcast_dynamic-update-slice_fusion, bf16[4096,1024]{1,0:T(8,128)(2,1)} %bitcast.29), kind=kOutput, calls=%fused_computation.2 | convolution fusion | flops 2148532224 | bytes 11010048 | tf_op jit(solution)/shard_map/dot_general | solution.py:103
  104.2 158.8 %reduce-scatter.7.cloned.1.call-done = bf16[128,1024]{1,0:T(8,128)(2,1)} async-done(((bf16[4096,1024]{1,0:T(8,128)(2,1)}), bf16[128,1024]{1,0:T(8,128)(2,1)}) %reduce-scatter.7.cloned.1.call-update) | async-done | bytes 262160
  263.0 1.1 copy.55
  264.1 1.0 copy.47
  265.1 47.3 %reduce-scatter.5.cloned.1.call-done = bf16[32,4096]{1,0:T(8,128)(2,1)} async-done(((bf16[256,4096]{1,0:T(8,128)(2,1)}), bf16[32,4096]{1,0:T(8,128)(2,1)}) %reduce-scatter.5.cloned.1.call-update) | async-done | bytes 262160 | tf_op jit(solution)/shard_map/reduce_scatter | solution.py:102
  (21 shorter events, 1.4 us)
Async XLA Ops:
  7.2 15.1 %copy-start = (bf16[1,256,512]{2,1,0:T(8,128)(2,1)S(1)}, bf16[1,256,512]{2,1,0:T(8,128)(2,1)}, u32[]{:S(2)}) copy-start(bf16[1,256,512]{2,1,0:T(8,128)(2,1)} %param.12) | copy-start | bytes 786436
  7.2 15.9 %copy-start.2 = (s32[1,256]{1,0:T(1,128)S(1)}, s32[1,256]{1,0:T(1,128)}, u32[]{:S(2)}) copy-start(s32[1,256]{1,0:T(1,128)} %param.13) | copy-start | bytes 3076
  9.8 60.1 %all-to-all-start = ((bf16[8,1,32,4096]{3,2,1,0:T(8,128)(2,1)}), bf16[8,1,32,4096]{3,2,1,0:T(8,128)(2,1)S(1)}, u32[]{:S(2)}, u32[]{:S(2)}) async-start(bf16[8,1,32,4096]{3,2,1,0:T(8,128)(2,1)} %stack.2), calls=%async_computation.1 | async-start | bytes 4194304 | tf_op jit(solution)/shard_map/all_to_all | solution.py:112
  18.2 244.8 %reduce-scatter.7.cloned.1.call-start = ((), (), s32[]{:S(2)}) async-start(), calls=%async_computation.4 | async-start | bytes 8650752
  23.0 4.0 %copy-start.1 = (bf16[2,128,4,128]{3,2,1,0:T(4,128)(2,1)S(1)}, bf16[2,128,4,128]{3,2,1,0:T(4,128)(2,1)}, u32[]{:S(2)}) copy-start(bf16[2,128,4,128]{3,2,1,0:T(4,128)(2,1)} %reshape_squeeze.9) | copy-start | bytes 786436
  87.5 224.9 %reduce-scatter.5.cloned.1.call-start = ((), (), s32[]{:S(2)}) async-start(), calls=%async_computation.3 | async-start | bytes 2359296 | tf_op jit(solution)/shard_map/reduce_scatter | solution.py:102
Sparse Core Ops, SparseCore 0:
  87.6 175.3 reduce-scatter.6
  266.1 46.2 reduce-scatter.4
